TPU v7x, 256 devices: a whole 4x4x8 slice. The times are simulated.
256 devices in a mesh: row: 32 (over z, y), col: 8 (over x, core).
Axes of the slice: x: 4, y: 4, z: 8, core: 2. Of those that a mesh axis runs over, the one named last changes fastest.
Arguments:
- feats: bfloat16 [131072, 256], P(('row', 'col')), may hold values from -6 to 6
- w_msg: bfloat16 [256, 256], replicated, may hold values from -0.375 to 0.375
- w_self: bfloat16 [256, 256], replicated, may hold values from -0.375 to 0.375
- bias: float32 [256], replicated, may hold values from -3 to 3
- hit_mask: int32 [131072], P(('row', 'col')), may hold values 0 or 1
- block_cols: int32 [32, 8, 96], P('row', 'col'), may hold values from 0 to 127, as said below
- block_count: int32 [32, 8], P('row', 'col'), may hold values from 32 to 96, as said below
- edge_vals: bfloat16 [32, 8, 96, 128, 128], P('row', 'col'), may hold values from -0.125 to 0.125
- grad_out: bfloat16 [131072, 256], P(('row', 'col')), may hold values from -3 to 3
Outputs:
- hidden: bfloat16 [131072, 256], P(('row', 'col'))
- grad_feats: bfloat16 [131072, 256], P(('row', 'col'))
- edge_grad: bfloat16 [32, 8, 96, 128, 128], P('row', 'col')
- w_msg_grad: float32 [256, 256], replicated
- w_self_grad: float32 [256, 256], replicated
- bias_grad: float32 [256], replicated
Inputs may be any that keep to these rules, and one draw needn't show every extreme that they name: `block_cols`: slot s of a tile serves the tile's local block row s % 32; the block columns of the slots that serve one block row of one tile are different. Slots from block_count on are unused.
All inputs are finite; a program needn't handle non-finite values. No bound on the sum of `hit_mask` on one device may be relied on, other than what follows from the above.
Results may differ from a plain program's by a relative error of at most 0.015.
Values may be sent and summed in bfloat16 or wider, within the bound.
A program may use at most 128 MiB of HBM per device.

v0:
```python
import math
import jax
import jax.numpy as jnp
from jax import lax
from jax.sharding import PartitionSpec as P


def activate(pre, row_mask, grad_in):
    sig = jax.nn.sigmoid(pre)
    hidden = (pre * sig * row_mask).astype(jnp.bfloat16)
    deriv = sig * (1.0 + pre * (1.0 - sig))
    grad_pre = (grad_in.astype(jnp.float32) * row_mask * deriv).astype(jnp.bfloat16)
    return (hidden, grad_pre)


def per_device(feats, w_msg, w_self, bias, hit_mask, block_cols, block_count, edge_vals, grad_out):
    row_count = lax.axis_size("row")
    col_count = lax.axis_size("col")
    own_rows = feats.shape[0]
    width = feats.shape[1]
    row_mask = hit_mask.astype(jnp.float32)[:, None]
    messages = (jnp.dot(feats, w_msg, preferred_element_type=jnp.float32) * row_mask).astype(
        jnp.bfloat16
    )
    column_msgs = lax.all_gather(messages, "row", axis=0, tiled=True)
    slot_cols = block_cols[0, 0]
    edge_block = edge_vals[0, 0]
    slot_total = edge_block.shape[0]
    edge_size = edge_block.shape[1]
    tile_rows = col_count * own_rows // edge_size
    tile_cols = row_count * own_rows // edge_size
    slot_depth = slot_total // tile_rows
    slot_flags = jnp.arange(slot_total, dtype=jnp.int32) < block_count[0, 0]
    edge_live = (edge_block * slot_flags.astype(jnp.bfloat16)[:, None, None]).reshape(
        slot_depth, tile_rows, edge_size, edge_size
    )
    col_blocks = column_msgs.reshape(tile_cols, edge_size, width)[slot_cols].reshape(
        slot_depth, tile_rows, edge_size, width
    )
    partial_value = jnp.einsum(
        "krij,krjf->rif", edge_live, col_blocks, preferred_element_type=jnp.float32
    ).reshape(tile_rows * edge_size, width)
    summed = lax.psum_scatter(
        partial_value.astype(jnp.bfloat16), "col", scatter_dimension=0, tiled=True
    ).astype(jnp.float32)
    pre = summed + jnp.dot(feats, w_self, preferred_element_type=jnp.float32) + bias
    hidden, grad_pre = activate(pre, row_mask, grad_out)
    grad_rows_all = lax.all_gather(grad_pre, "col", axis=0, tiled=True)
    grad_tile = grad_rows_all.reshape(tile_rows, edge_size, width)
    backward = jnp.einsum(
        "krij,rif->krjf", edge_live, grad_tile, preferred_element_type=jnp.float32
    ).reshape(slot_total, edge_size, width)
    back_part = jax.ops.segment_sum(backward, slot_cols, num_segments=tile_cols).reshape(
        tile_cols * edge_size, width
    )
    edge_grad = (
        jnp.einsum(
            "rif,krjf->krij", grad_tile, col_blocks, preferred_element_type=jnp.float32
        ).reshape(slot_total, edge_size, edge_size)
        * slot_flags.astype(jnp.float32)[:, None, None]
    ).astype(jnp.bfloat16)
    grad_sum = lax.psum_scatter(
        back_part.astype(jnp.bfloat16), "row", scatter_dimension=0, tiled=True
    ).astype(jnp.float32)
    grad_msg = (grad_sum * row_mask).astype(jnp.bfloat16)
    grad_feats = (
        jnp.einsum("hg,fg->hf", grad_msg, w_msg, preferred_element_type=jnp.float32)
        + jnp.einsum("hg,fg->hf", grad_pre, w_self, preferred_element_type=jnp.float32)
    ).astype(jnp.bfloat16)
    local_msg = jnp.einsum("hf,hg->fg", feats, grad_msg, preferred_element_type=jnp.float32)
    local_self = jnp.einsum("hf,hg->fg", feats, grad_pre, preferred_element_type=jnp.float32)
    local_bias = jnp.sum(grad_pre.astype(jnp.float32), axis=0)
    total_msg, total_self, total_bias = lax.psum(
        (local_msg, local_self, local_bias), ("row", "col")
    )
    factor = 1.0 / math.sqrt(own_rows * row_count * col_count)
    return (
        hidden,
        grad_feats,
        edge_grad[None, None],
        total_msg * factor,
        total_self * factor,
        total_bias * factor,
    )


def solution(mesh):
    placed = (
        P(("row", "col"), None),
        P(),
        P(),
        P(),
        P(("row", "col")),
        P("row", "col", None),
        P("row", "col"),
        P("row", "col", None, None, None),
        P(("row", "col"), None),
    )
    return jax.shard_map(
        per_device,
        mesh=mesh,
        in_specs=placed,
        out_specs=(
            P(("row", "col"), None),
            P(("row", "col"), None),
            P("row", "col", None, None, None),
            P(),
            P(),
            P(),
        ),
        check_vma=False,
    )
```

profile of v0, /device:TPU:2, one launch (start us, length us, event | category | flops | bytes accessed | tf_op | source)
XLA Modules:
  0.0 757.9 jit_solution(17679265204071514697)
XLA Ops:
  7.2 0.7 convert_element_type.67
  7.9 0.2 copy-done
  8.1 1.8 fusion.12
  10.0 0.0 reduce-scatter.3.cloned.1.call-start
  10.7 0.7 fusion.16
  11.4 100.7 %all-gather.3.cloned.1.call-done = bf16[16384,256]{1,0:T(8,128)(2,1)} async-done(((bf16[512,256]{1,0:T(8,128)(2,1)}), bf16[16384,256]{1,0:T(8,128)(2,1)}) %all-gather.3.cloned.1.call-update) | async-done | bytes 8388624 | tf_op jit(solution)/shard_map/all_gather | solution.py:25
  112.0 9.5 %gather_fusion = bf16[96,128,256]{2,1,0:T(8,128)(2,1)} fusion(bf16[128,128,256]{2,1,0:T(8,128)(2,1)} %bitcast.53, s32[1024]{0:T(1024)S(1)} %pad_clamp_fusion), kind=kCustom, calls=%fused_computation | custom fusion | bytes 12583296 | tf_op jit(solution)/shard_map/gather | solution.py:37
  121.5 5.5 bitcast_convert_fusion
  127.0 0.0 all-gather.5.cloned.1.call-start
  127.1 30.4 %reduce-scatter.3.cloned.1.call-done = bf16[512,256]{1,0:T(8,128)(2,1)} async-done(((bf16[4096,256]{1,0:T(8,128)(2,1)}), bf16[512,256]{1,0:T(8,128)(2,1)}) %reduce-scatter.3.cloned.1.call-update) | async-done | bytes 262160 | tf_op jit(solution)/shard_map/reduce_scatter | solution.py:43
  157.5 2.3 convert_reduce_fusion
  159.8 0.0 reduce-scatter.5.cloned.1.call-start
  159.9 28.7 %all-gather.5.cloned.1.call-done = bf16[4096,256]{1,0:T(8,128)(2,1)} async-done(((bf16[512,256]{1,0:T(8,128)(2,1)}), bf16[4096,256]{1,0:T(8,128)(2,1)}) %all-gather.5.cloned.1.call-update) | async-done | bytes 2097168 | tf_op jit(solution)/shard_map/all_gather | solution.py:48
  188.6 8.0 %convolution_bitcast_fusion = f32[3,32,128,256]{2,3,0,1:T(8,128)} fusion(bf16[32,128,256,1]{2,1,3,0:T(8,128)(2,1)} %bitcast.51, bf16[3,32,128,128]{3,2,1,0:T(8,128)(2,1)S(1)} %bitcast.55, bf16[3,32]{0,1:T(8,128)(2,1)S(1)} %fusion.15), kind=kOutput, calls=%fused_computation.7 | convolution fusion | flops 811597824 | bytes 17825984 | tf_op jit(solution)/shard_map/krij,rif->krjf/dot_general | solution.py:50
  196.6 12.6 %copy.22 = f32[3,32,128,256]{3,2,1,0:T(8,128)} copy(f32[3,32,128,256]{2,3,0,1:T(8,128)} %convolution_bitcast_fusion) | data formatting | bytes 25165824 | tf_op jit(solution)/shard_map/krij,rif->krjf/transpose | solution.py:50
  209.2 7.8 %broadcast_in_dim.2 = f32[128,128,256]{2,1,0:T(8,128)} broadcast(f32[]{:T(128)} %constant.4.clone.1), dimensions={} | broadcast | bytes 16777220 | tf_op jit(solution)/shard_map/broadcast_in_dim | solution.py:53
  217.0 29.1 %scatter_fusion = f32[128,128,256]{2,1,0:T(8,128)} fusion(f32[128,128,256]{2,1,0:T(8,128)} %broadcast_in_dim.2, s32[96]{0:T(128)S(1)} %bitcast.57, f32[96,128,256]{2,1,0:T(8,128)} %bitcast.46), kind=kCustom, calls=%fused_computation.1 | custom fusion | flops 3145728 | bytes 37749120 | tf_op jit(solution)/shard_map/scatter-add | solution.py:53
  246.1 9.0 %convert_element_type.75 = bf16[128,128,256]{2,1,0:T(8,128)(2,1)} convert(f32[128,128,256]{2,1,0:T(8,128)} %scatter_fusion) | non-fusion elementwise | flops 4194304 | bytes 25165824 | tf_op jit(solution)/shard_map/convert_element_type | solution.py:63
  255.2 78.1 %psum.23 = f32[256]{0:T(256)S(1)} all-reduce(f32[256]{0:T(256)S(1)} %get-tuple-element.20), channel_id=1, replica_groups=mesh['row'=32,'col'=8] {'row','col'}, use_global_device_ids=true, to_apply=%region_6.0 | all-reduce | flops 256 | bytes 2048 | tf_op jit(solution)/shard_map/psum | solution.py:73
  333.3 0.6 broadcast_multiply_fusion.2
  333.9 1.0 convolution_bitcast_fusion.1
  334.9 7.3 fusion.4
  342.1 6.6 copy.24
  348.7 5.1 multiply_convert_fusion
  353.8 134.4 %reduce-scatter.5.cloned.1.call-done = bf16[512,256]{1,0:T(8,128)(2,1)} async-done(((bf16[16384,256]{1,0:T(8,128)(2,1)}), bf16[512,256]{1,0:T(8,128)(2,1)}) %reduce-scatter.5.cloned.1.call-update) | async-done | bytes 262160 | tf_op jit(solution)/shard_map/reduce_scatter | solution.py:62
  488.2 2.0 convolution_bitcast_fusion.2
  490.2 1.2 fusion.14
  491.4 1.0 fusion.13
  492.4 256.2 %all-reduce.3.cloned.1.call-done = (f32[256,256]{0,1:T(8,128)}, f32[256,256]{0,1:T(8,128)}) async-done(((f32[256,256]{0,1:T(8,128)}, f32[256,256]{0,1:T(8,128)}), (f32[256,256]{0,1:T(8,128)}, f32[256,256]{0,1:T(8,128)})) %all-reduce.3.cloned.1.call-update) | async-done | bytes 524304 | tf_op jit(solution)/shard_map/psum | solution.py:73
  748.6 1.1 broadcast_multiply_fusion
  749.7 0.8 copy.26
  750.5 0.8 copy.25
  (23 shorter events, 0.2 us)
Async XLA Ops:
  7.2 1.0 copy-start
  7.2 104.8 %all-gather.3.cloned.1.call-start = ((), (), s32[]{:S(2)}) async-start(), calls=%async_computation.2 | async-start | bytes 8650752 | tf_op jit(solution)/shard_map/all_gather | solution.py:25
  10.0 147.5 %reduce-scatter.3.cloned.1.call-start = ((), (), s32[]{:S(2)}) async-start(), calls=%async_computation.3 | async-start | bytes 2359296 | tf_op jit(solution)/shard_map/reduce_scatter | solution.py:43
  112.0 9.5 %copy-start.2 = (bf16[1,1,96,128,128]{4,3,2,1,0:T(8,128)(2,1)S(1)}, bf16[1,1,96,128,128]{4,3,2,1,0:T(8,128)(2,1)}, u32[]{:S(2)}) copy-start(bf16[1,1,96,128,128]{4,3,2,1,0:T(8,128)(2,1)} %param.16) | copy-start | bytes 9437188
  121.5 36.0 %copy-start.5 = (bf16[256,256]{1,0:T(8,128)(2,1)S(1)}, bf16[256,256]{1,0:T(8,128)(2,1)}, u32[]{:S(2)}) copy-start(bf16[256,256]{1,0:T(8,128)(2,1)} %param.11) | copy-start | bytes 393220
  127.0 61.6 %all-gather.5.cloned.1.call-start = ((), (), s32[]{:S(2)}) async-start(), calls=%async_computation.4 | async-start | bytes 2359296 | tf_op jit(solution)/shard_map/all_gather | solution.py:48
  159.8 328.4 %reduce-scatter.5.cloned.1.call-start = ((), (), s32[]{:S(2)}) async-start(), calls=%async_computation.5 | async-start | bytes 8650752 | tf_op jit(solution)/shard_map/reduce_scatter | solution.py:62
  209.2 7.9 %copy-start.6 = (s32[1,1,96]{2,1,0:T(1,128)S(1)}, s32[1,1,96]{2,1,0:T(1,128)}, u32[]{:S(2)}) copy-start(s32[1,1,96]{2,1,0:T(1,128)} %param.14) | copy-start | bytes 1156
  255.1 78.7 %copy-start.3 = (bf16[512,256]{1,0:T(8,128)(2,1)S(1)}, bf16[512,256]{1,0:T(8,128)(2,1)}, u32[]{:S(2)}) copy-start(bf16[512,256]{1,0:T(8,128)(2,1)} %get-tuple-element.21) | copy-start | bytes 786436
  255.1 79.7 %copy-start.1 = (bf16[4096,256]{1,0:T(8,128)(2,1)S(1)}, bf16[4096,256]{1,0:T(8,128)(2,1)}, u32[]{:S(2)}) copy-start(bf16[4096,256]{1,0:T(8,128)(2,1)} %all-gather.5.cloned.1.call-done) | copy-start | bytes 6291460
  255.2 493.4 %all-reduce.3.cloned.1.call-start = ((), (), s32[]{:S(2)}) async-start(), calls=%async_computation.6 | async-start | bytes 1048576 | tf_op jit(solution)/shard_map/psum | solution.py:73
  348.7 141.5 %copy-start.4 = (bf16[256,256]{1,0:T(8,128)(2,1)S(1)}, bf16[256,256]{1,0:T(8,128)(2,1)}, u32[]{:S(2)}) copy-start(bf16[256,256]{1,0:T(8,128)(2,1)} %param.10) | copy-start | bytes 393220
Sparse Core Ops, SparseCore 0:
  11.1 100.8 all-gather.2
  127.1 30.3 reduce-scatter.2
  159.9 28.6 all-gather.4
  255.3 232.8 reduce-scatter.4
  494.2 254.3 all-reduce.2
where the time goes:
time: 758 us
  waiting for transfers between devices  550 us (73%)
  blocking collectives  78.1 us (10%)
  other arithmetic  46.2 us (6%)
  local copies, waits for them, and re-layouts  38.4 us (5%)
  matrix products  30 us (4%)
  between operations  14.5 us (2%)
    psum x1, waiting for transfers between devices, per_device(): lax.psum((local_msg, local_self, local_bias), ('row', 'col'))  256 us
    reduce_scatter x1, waiting for transfers between devices, per_device(): lax.psum_scatter(back_part.astype(jnp.bfloat16), 'row', scatter_dimension...  134 us
    all_gather x1, waiting for transfers between devices, per_device(): column_msgs = lax.all_gather(messages, 'row', axis=0, tiled=True)  101 us
    psum x1, blocking collectives, per_device(): lax.psum((local_msg, local_self, local_bias), ('row', 'col'))  78.1 us
    reduce_scatter x1, waiting for transfers between devices, per_device(): lax.psum_scatter(partial_value.astype(jnp.bfloat16), 'col', scatter_dimen...  30.4 us
    scatter-add x1, other arithmetic, per_device(): jax.ops.segment_sum(backward, slot_cols, num_segments=tile_cols)  29.1 us
    all_gather x1, waiting for transfers between devices, per_device(): grad_rows_all = lax.all_gather(grad_pre, 'col', axis=0, tiled=True)  28.7 us
  transfers between devices with their start and end apart: 5, of which 5 were waited for; matrix products, arithmetic and copies ran while one was open for 3% of the time, Pallas kernels for 0%

commit v1 on v0

--- a/solution.py
+++ b/solution.py
@@ -22,7 +22,9 @@
     messages = (jnp.dot(feats, w_msg, preferred_element_type=jnp.float32) * row_mask).astype(
         jnp.bfloat16
     )
-    column_msgs = lax.all_gather(messages, "row", axis=0, tiled=True)
+    column_msgs = jnp.concatenate(
+        lax.all_to_all(jnp.stack([messages] * lax.axis_size("row")), "row", 0, 0), axis=0
+    )
     slot_cols = block_cols[0, 0]
     edge_block = edge_vals[0, 0]
     slot_total = edge_block.shape[0]

time: 758 us -> 869 us (1.15)
  waiting for transfers between devices: 550 us -> 647 us
  starting transfers between devices: 0.21 us -> 11.9 us
    all_to_all x0 -> x1, waiting for transfers between devices: none -> 188 us  [per_device(): lax.all_to_all(jnp.stack([messages] * lax.axis_size('row')), 'row', 0, 0)]
    all_gather x1 -> x0, waiting for transfers between devices: 101 us -> none  [per_device(): column_msgs = lax.all_gather(messages, 'row', axis=0, tiled=True)]
    all_to_all x0 -> x1, starting transfers between devices: none -> 11.7 us  [per_device(): lax.all_to_all(jnp.stack([messages] * lax.axis_size('row')), 'row', 0, 0)]
    reduce_scatter x1, waiting for transfers between devices: 30.4 us -> 39.5 us  [per_device(): lax.psum_scatter(partial_value.astype(jnp.bfloat16), 'col', scatter_dimen...]
where the time goes in v1:
time: 869 us; the launch traced here: 868 us
  waiting for transfers between devices  647 us (74%)
  blocking collectives  77.9 us (9%)
  other arithmetic  45.6 us (5%)
  local copies, waits for them, and re-layouts  42.6 us (5%)
  matrix products  29.3 us (3%)
  between operations  14.5 us (2%)
  starting transfers between devices  11.9 us (1%)
    psum x1, waiting for transfers between devices, per_device(): lax.psum((local_msg, local_self, local_bias), ('row', 'col'))  256 us
    all_to_all x1, waiting for transfers between devices, per_device(): lax.all_to_all(jnp.stack([messages] * lax.axis_size('row')), 'row', 0, 0)  188 us
    reduce_scatter x1, waiting for transfers between devices, per_device(): lax.psum_scatter(back_part.astype(jnp.bfloat16), 'row', scatter_dimension...  135 us
    psum x1, blocking collectives, per_device(): lax.psum((local_msg, local_self, local_bias), ('row', 'col'))  77.9 us
    reduce_scatter x1, waiting for transfers between devices, per_device(): lax.psum_scatter(partial_value.astype(jnp.bfloat16), 'col', scatter_dimen...  39.5 us
    scatter-add x1, other arithmetic, per_device(): jax.ops.segment_sum(backward, slot_cols, num_segments=tile_cols)  29.1 us
    all_gather x1, waiting for transfers between devices, per_device(): grad_rows_all = lax.all_gather(grad_pre, 'col', axis=0, tiled=True)  28.8 us
  transfers between devices with their start and end apart: 5, of which 5 were waited for; matrix products, arithmetic and copies ran while one was open for 3% of the time, Pallas kernels for 0%

profile of v1, /device:TPU:2, one launch (start us, length us, event | category | flops | bytes accessed | tf_op | source)
XLA Modules:
  0.0 868.4 jit_solution(7515058434217326650)
XLA Ops:
  7.2 0.7 convert_element_type.67
  7.9 0.2 copy-done
  8.1 1.1 fusion.12
  9.3 4.2 stack.2
  13.5 11.7 %all-to-all-start = ((bf16[32,512,256]{2,1,0:T(8,128)(2,1)}), bf16[32,512,256]{2,1,0:T(8,128)(2,1)}, u32[]{:S(2)}, u32[]{:S(2)}) async-start(bf16[32,512,256]{2,1,0:T(8,128)(2,1)} %stack.2), calls=%async_computation | async-start | bytes 16777216 | tf_op jit(solution)/shard_map/all_to_all | solution.py:26
  26.0 187.6 %all-to-all-done = bf16[32,512,256]{2,1,0:T(8,128)(2,1)} async-done(((bf16[32,512,256]{2,1,0:T(8,128)(2,1)}), bf16[32,512,256]{2,1,0:T(8,128)(2,1)}, u32[]{:S(2)}, u32[]{:S(2)}) %all-to-all-start) | async-done | bytes 8388640 | tf_op jit(solution)/shard_map/all_to_all | solution.py:26
  213.6 9.5 %gather_fusion = bf16[96,128,256]{2,1,0:T(8,128)(2,1)} fusion(bf16[128,128,256]{2,1,0:T(8,128)(2,1)} %bitcast.2, s32[1024]{0:T(1024)S(1)} %pad_clamp_fusion), kind=kCustom, calls=%fused_computation | custom fusion | bytes 12583296 | tf_op jit(solution)/shard_map/gather | solution.py:39
  223.1 5.5 bitcast_convert_fusion
  228.6 0.0 all-gather.2.cloned.1.call-start
  228.6 39.5 %reduce-scatter.3.cloned.1.call-done = bf16[512,256]{1,0:T(8,128)(2,1)} async-done(((bf16[4096,256]{1,0:T(8,128)(2,1)}), bf16[512,256]{1,0:T(8,128)(2,1)}) %reduce-scatter.3.cloned.1.call-update) | async-done | bytes 262160 | tf_op jit(solution)/shard_map/reduce_scatter | solution.py:45
  268.1 2.3 convert_reduce_fusion
  270.5 0.0 reduce-scatter.5.cloned.1.call-start
  270.5 28.8 %all-gather.2.cloned.1.call-done = bf16[4096,256]{1,0:T(8,128)(2,1)} async-done(((bf16[512,256]{1,0:T(8,128)(2,1)}), bf16[4096,256]{1,0:T(8,128)(2,1)}) %all-gather.2.cloned.1.call-update) | async-done | bytes 2097168 | tf_op jit(solution)/shard_map/all_gather | solution.py:50
  299.4 8.0 convolution_bitcast_fusion
  307.3 12.6 %copy.22 = f32[3,32,128,256]{3,2,1,0:T(8,128)} copy(f32[3,32,128,256]{2,3,0,1:T(8,128)} %convolution_bitcast_fusion) | data formatting | bytes 25165824 | tf_op jit(solution)/shard_map/krij,rif->krjf/transpose | solution.py:52
  320.0 7.8 broadcast_in_dim.2
  327.8 29.1 %scatter_fusion = f32[128,128,256]{2,1,0:T(8,128)} fusion(f32[128,128,256]{2,1,0:T(8,128)} %broadcast_in_dim.2, s32[96]{0:T(128)S(1)} %bitcast.56, f32[96,128,256]{2,1,0:T(8,128)} %bitcast.46), kind=kCustom, calls=%fused_computation.1 | custom fusion | flops 3145728 | bytes 37749120 | tf_op jit(solution)/shard_map/scatter-add | solution.py:55
  356.9 9.0 %convert_element_type.75 = bf16[128,128,256]{2,1,0:T(8,128)(2,1)} convert(f32[128,128,256]{2,1,0:T(8,128)} %scatter_fusion) | non-fusion elementwise | flops 4194304 | bytes 25165824 | tf_op jit(solution)/shard_map/convert_element_type | solution.py:65
  366.0 77.9 %psum.23 = f32[256]{0:T(256)S(1)} all-reduce(f32[256]{0:T(256)S(1)} %get-tuple-element.20), channel_id=1, replica_groups=mesh['row'=32,'col'=8] {'row','col'}, use_global_device_ids=true, to_apply=%region_6.0 | all-reduce | flops 256 | bytes 2048 | tf_op jit(solution)/shard_map/psum | solution.py:75
  443.9 0.6 broadcast_multiply_fusion.2
  444.5 1.0 convolution_bitcast_fusion.1
  445.4 7.3 fusion.4
  452.7 6.6 copy.24
  459.3 5.1 multiply_convert_fusion
  464.4 134.5 %reduce-scatter.5.cloned.1.call-done = bf16[512,256]{1,0:T(8,128)(2,1)} async-done(((bf16[16384,256]{1,0:T(8,128)(2,1)}), bf16[512,256]{1,0:T(8,128)(2,1)}) %reduce-scatter.5.cloned.1.call-update) | async-done | bytes 262160 | tf_op jit(solution)/shard_map/reduce_scatter | solution.py:64
  598.9 2.0 convolution_bitcast_fusion.2
  601.0 1.2 fusion.14
  602.2 1.0 fusion.13
  603.1 255.9 %all-reduce.3.cloned.1.call-done = (f32[256,256]{0,1:T(8,128)}, f32[256,256]{0,1:T(8,128)}) async-done(((f32[256,256]{0,1:T(8,128)}, f32[256,256]{0,1:T(8,128)}), (f32[256,256]{0,1:T(8,128)}, f32[256,256]{0,1:T(8,128)})) %all-reduce.3.cloned.1.call-update) | async-done | bytes 524304 | tf_op jit(solution)/shard_map/psum | solution.py:75
  859.1 1.1 broadcast_multiply_fusion
  860.2 0.8 copy.26
  861.0 0.8 copy.25
  (25 shorter events, 0.2 us)
Async XLA Ops:
  7.2 1.0 copy-start
  13.5 12.5 %copy-start.6 = (s32[1,1,96]{2,1,0:T(1,128)S(1)}, s32[1,1,96]{2,1,0:T(1,128)}, u32[]{:S(2)}) copy-start(s32[1,1,96]{2,1,0:T(1,128)} %param.14) | copy-start | bytes 1156
  13.5 200.1 %all-to-all-start = ((bf16[32,512,256]{2,1,0:T(8,128)(2,1)}), bf16[32,512,256]{2,1,0:T(8,128)(2,1)}, u32[]{:S(2)}, u32[]{:S(2)}) async-start(bf16[32,512,256]{2,1,0:T(8,128)(2,1)} %stack.2), calls=%async_computation | async-start | bytes 16777216 | tf_op jit(solution)/shard_map/all_to_all | solution.py:26
  25.2 242.9 %reduce-scatter.3.cloned.1.call-start = ((), (), s32[]{:S(2)}) async-start(), calls=%async_computation.3 | async-start | bytes 2359296 | tf_op jit(solution)/shard_map/reduce_scatter | solution.py:45
  213.6 9.5 %copy-start.2 = (bf16[1,1,96,128,128]{4,3,2,1,0:T(8,128)(2,1)S(1)}, bf16[1,1,96,128,128]{4,3,2,1,0:T(8,128)(2,1)}, u32[]{:S(2)}) copy-start(bf16[1,1,96,128,128]{4,3,2,1,0:T(8,128)(2,1)} %param.16) | copy-start | bytes 9437188
  223.1 45.1 %copy-start.5 = (bf16[256,256]{1,0:T(8,128)(2,1)S(1)}, bf16[256,256]{1,0:T(8,128)(2,1)}, u32[]{:S(2)}) copy-start(bf16[256,256]{1,0:T(8,128)(2,1)} %param.11) | copy-start | bytes 393220
  228.6 70.8 %all-gather.2.cloned.1.call-start = ((), (), s32[]{:S(2)}) async-start(), calls=%async_computation.4 | async-start | bytes 2359296 | tf_op jit(solution)/shard_map/all_gather | solution.py:50
  270.5 328.4 %reduce-scatter.5.cloned.1.call-start = ((), (), s32[]{:S(2)}) async-start(), calls=%async_computation.5 | async-start | bytes 8650752 | tf_op jit(solution)/shard_map/reduce_scatter | solution.py:64
  320.0 7.9 copy-start.7
  365.9 78.6 %copy-start.3 = (bf16[512,256]{1,0:T(8,128)(2,1)S(1)}, bf16[512,256]{1,0:T(8,128)(2,1)}, u32[]{:S(2)}) copy-start(bf16[512,256]{1,0:T(8,128)(2,1)} %get-tuple-element.21) | copy-start | bytes 786436
  365.9 79.5 %copy-start.1 = (bf16[4096,256]{1,0:T(8,128)(2,1)S(1)}, bf16[4096,256]{1,0:T(8,128)(2,1)}, u32[]{:S(2)}) copy-start(bf16[4096,256]{1,0:T(8,128)(2,1)} %all-gather.2.cloned.1.call-done) | copy-start | bytes 6291460
  365.9 493.2 %all-reduce.3.cloned.1.call-start = ((), (), s32[]{:S(2)}) async-start(), calls=%async_computation.6 | async-start | bytes 1048576 | tf_op jit(solution)/shard_map/psum | solution.py:75
  459.3 141.7 %copy-start.4 = (bf16[256,256]{1,0:T(8,128)(2,1)S(1)}, bf16[256,256]{1,0:T(8,128)(2,1)}, u32[]{:S(2)}) copy-start(bf16[256,256]{1,0:T(8,128)(2,1)} %param.10) | copy-start | bytes 393220
Sparse Core Ops, SparseCore 0:
  228.7 39.4 reduce-scatter.2
  270.6 28.7 all-gather.1
  366.1 232.8 reduce-scatter.4
  605.0 254.0 all-reduce.2
